TPU v7x, 128 devices: a whole 4x4x4 slice. The times are simulated.
128 devices in a mesh: ctx: 32 (over z, x, core), head: 4 (over y).
Axes of the slice: x: 4, y: 4, z: 4, core: 2. Of those that a mesh axis runs over, the one named last changes fastest.
Arguments:
- queries: bfloat16 [16384, 4096], P('ctx', 'head'), may hold values from -8 to 8
- keys: bfloat16 [16384, 512], P('ctx', 'head'), may hold values from -8 to 8
- values: bfloat16 [16384, 512], P('ctx', 'head'), may hold values from -6 to 6
- distances: int32 [4, 3], P('head'), may hold values from 1 to 31, as said below
- out_weight: bfloat16 [4096, 2048], P('head'), may hold values from -0.09375 to 0.09375
- residual: bfloat16 [16384, 2048], P(('ctx', 'head')), may hold values from -6 to 6
- norm_gain: float32 [2048], replicated, may hold values from 0.25 to 1.75
- expert_gate_up: bfloat16 [128, 2048, 1536], P(('ctx', 'head')), may hold values from -0.125 to 0.125
- expert_down: bfloat16 [128, 768, 2048], P(('ctx', 'head')), may hold values from -0.21875 to 0.21875
- routes: int32 [16384, 8], P(('ctx', 'head')), may hold values from 0 to 127, all different within a row; in each aligned block of 128 rows (0 to 127, 128 to 255, ...) at most 16 rows name the same one
- route_weights: float32 [16384, 8], P(('ctx', 'head')), may hold values from 0.05 to 0.5
Outputs:
- attended: bfloat16 [16384, 2048], P(('ctx', 'head'))
- moe_out: bfloat16 [16384, 2048], P(('ctx', 'head'))
Inputs may be any that keep to these rules, and one draw needn't show every extreme that they name: Each row holds 3 different distances; some row holds the distance 16384 // 1024. `routes`: among the 128 rows of one device, no expert is named by more than 16 rows.
All inputs are finite; a program needn't handle non-finite values.
Results may differ from a plain program's by a relative error of at most 0.01.
Values may be sent and summed in bfloat16 or wider, within the bound.
No kernel may reach another device: no remote copies, remote signals or barrier semaphores. Data moves between devices by JAX's collectives and lax.ppermute only.
A program may use at most 128 MiB of HBM per device.

v0:
```python
import math
import jax
import jax.numpy as jnp
from jax import lax
from jax.sharding import PartitionSpec as P

HD = 128
FFE = 768
TOP = 8
EXP_DEV = 1
BLK = 128
DIST = 3


def expert_rows(arrived, expert_gate_up, expert_down, sources):
    width = arrived.shape[2]
    grid = arrived.reshape(sources, EXP_DEV, arrived.shape[1], width)
    projected = jnp.einsum(
        "sekd,edf->eskf", grid, expert_gate_up, preferred_element_type=jnp.float32
    )
    hidden = (jax.nn.silu(projected[..., :FFE]) * projected[..., FFE:]).astype(jnp.bfloat16)
    output = jnp.einsum("eskf,efd->sekd", hidden, expert_down, preferred_element_type=jnp.float32)
    return output.astype(jnp.bfloat16).reshape(arrived.shape)


def body(
    queries,
    keys,
    values,
    distances,
    out_weight,
    residual,
    norm_gain,
    expert_gate_up,
    expert_down,
    routes,
    route_weights,
):
    length = queries.shape[0]
    groups = queries.shape[1] // HD
    blocks = length // BLK
    scale = 1.0 / math.sqrt(HD)
    wanted = distances[0]
    source = lax.axis_index("ctx") - wanted
    usable = source >= 0
    packed = jnp.concatenate([keys, values], axis=1)
    everything = lax.all_gather(packed, "ctx", axis=0, tiled=True)
    offsets = jnp.maximum(source, 0) * length
    fetched = jnp.stack(
        [
            lax.dynamic_slice_in_dim(everything, offsets[slot_index], length, 0)
            for slot_index in range(DIST)
        ]
    )
    query = queries.reshape(length, groups, HD)
    causal = jnp.arange(length)[:, None] >= jnp.arange(length)[None, :]
    local = jnp.einsum("tgd,ud->gtu", query, keys, preferred_element_type=jnp.float32) * scale
    local = jnp.where(causal[None], local, -jnp.inf)
    far_keys = fetched[:, :, :HD].reshape(DIST, blocks, BLK, HD)
    far_values = fetched[:, :, HD:].reshape(DIST, blocks, BLK, HD)
    query_blocks = queries.reshape(blocks, BLK, groups, HD)
    remote = (
        jnp.einsum("bqgd,jbud->gjbqu", query_blocks, far_keys, preferred_element_type=jnp.float32)
        * scale
    )
    remote = jnp.where(usable[None, :, None, None, None], remote, -jnp.inf)
    highest = jnp.maximum(local.max(-1), remote.max(axis=(1, 4)).reshape(groups, length))
    near_weight = jnp.exp(local - highest[:, :, None])
    far_weight = jnp.exp(remote - highest.reshape(groups, blocks, BLK)[:, None, :, :, None])
    denominator = near_weight.sum(-1) + far_weight.sum(axis=(1, 4)).reshape(groups, length)
    mixed = jnp.einsum(
        "gtu,ud->tgd", near_weight.astype(jnp.bfloat16), values, preferred_element_type=jnp.float32
    )
    far_mixed = jnp.einsum(
        "gjbqu,jbud->bqgd",
        far_weight.astype(jnp.bfloat16),
        far_values,
        preferred_element_type=jnp.float32,
    )
    mixed = mixed + far_mixed.reshape(length, groups, HD)
    attention = (
        (mixed / jnp.transpose(denominator)[:, :, None])
        .astype(jnp.bfloat16)
        .reshape(length, groups * HD)
    )
    summed = lax.psum_scatter(
        jnp.dot(attention, out_weight, preferred_element_type=jnp.float32),
        "head",
        scatter_dimension=0,
        tiled=True,
    )
    attended = (residual.astype(jnp.float32) + summed).astype(jnp.bfloat16)
    widened = attended.astype(jnp.float32)
    inverse = lax.rsqrt(jnp.mean(widened * widened, axis=-1, keepdims=True) + 1e-06)
    normed = (widened * inverse * norm_gain).astype(jnp.bfloat16)
    local_rows = normed.shape[0]
    width = normed.shape[1]
    devices = lax.axis_size(("ctx", "head"))
    experts = devices * EXP_DEV
    capacity = max(2, 2 * local_rows * TOP // experts)
    flat_experts = routes.reshape(local_rows * TOP)
    onehot = (flat_experts[:, None] == jnp.arange(experts, dtype=jnp.int32)[None, :]).astype(
        jnp.int32
    )
    places = jnp.sum(jnp.cumsum(onehot, axis=0) * onehot, axis=1) - 1
    owners = jnp.arange(local_rows * TOP, dtype=jnp.int32) // TOP
    outgoing = (
        jnp.zeros((experts, capacity, width), jnp.bfloat16)
        .at[flat_experts, places]
        .set(normed[owners])
    )
    answered = expert_rows(
        lax.all_to_all(outgoing, ("ctx", "head"), split_axis=0, concat_axis=0, tiled=True),
        expert_gate_up,
        expert_down,
        devices,
    )
    returned = lax.all_to_all(answered, ("ctx", "head"), split_axis=0, concat_axis=0, tiled=True)
    picked = returned[flat_experts, places].astype(jnp.float32)
    weighted = route_weights.reshape(local_rows * TOP)[:, None] * picked
    moe_out = weighted.reshape(local_rows, TOP, width).sum(axis=1).astype(jnp.bfloat16)
    return (attended, moe_out)


def solution(mesh):
    return jax.shard_map(
        body,
        mesh=mesh,
        in_specs=(
            P("ctx", "head"),
            P("ctx", "head"),
            P("ctx", "head"),
            P("head", None),
            P("head", None),
            P(("ctx", "head"), None),
            P(),
            P(("ctx", "head"), None, None),
            P(("ctx", "head"), None, None),
            P(("ctx", "head"), None),
            P(("ctx", "head"), None),
        ),
        out_specs=(P(("ctx", "head"), None), P(("ctx", "head"), None)),
        check_vma=False,
    )
```

profile of v0, /device:TPU:7, one launch (start us, length us, event | category | flops | bytes accessed | tf_op | source)
XLA Modules:
  0.0 481.5 jit_solution(17237951945180817351)
XLA Ops:
  7.2 1.9 pad_maximum_fusion.1
  14.4 2.6 copy.69
  19.7 2.3 bitcast_bitcast_fusion
  21.9 6.0 %fusion.8 = (f32[8,512]{1,0:T(8,128)S(1)}, f32[512,512,8]{1,0,2:T(8,128)}) fusion(pred[512,512]{0,1:T(8,128)(4,1)S(1)} %iota_compare_fusion, bf16[512,128]{1,0:T(8,128)(2,1)} %param.12, bf16[512,1024]{1,0:T(8,128)(2,1)} %param.11), kind=kOutput, calls=%fused_computation.12 | convolution fusion | flops 543158272 | bytes 9846784 | tf_op jit(solution)/shard_map/tgd,ud->gtu/dot_general | solution.py:57
  27.9 38.7 %all-gather.2.cloned.1.call-done = bf16[16384,256]{1,0:T(8,128)(2,1)} async-done(((bf16[512,256]{1,0:T(8,128)(2,1)}), bf16[16384,256]{1,0:T(8,128)(2,1)}) %all-gather.2.cloned.1.call-update) | async-done | bytes 8388624 | tf_op jit(solution)/shard_map/all_gather | solution.py:47
  68.3 2.2 bitcast_reduce_fusion
  70.5 2.2 fusion.12
  72.7 2.5 fusion.27
  75.2 3.2 copy.44
  78.4 3.1 reshape.226
  81.5 5.3 %fusion.3 = f32[8,512]{1,0:T(8,128)S(1)} fusion(f32[512,512,8]{1,0,2:T(8,128)} %get-tuple-element.22, f32[8,512]{1,0:T(8,128)S(1)} %bitcast_maximum_fusion.1, pred[512,512]{0,1:T(8,128)(4,1)S(1)} %iota_compare_fusion), kind=kLoop, calls=%fused_computation.9 | loop fusion | flops 8384512 | bytes 8683520 | tf_op jit(solution)/shard_map/reduce_sum | solution.py:70
  86.8 5.7 %fusion.26 = bf16[512,8,128]{0,2,1:T(8,128)(2,1)S(1)} fusion(f32[512,8,128]{0,2,1:T(8,128)S(1)} %copy-done.4, f32[512,512,8]{1,0,2:T(8,128)} %get-tuple-element.22, f32[8,512]{1,0:T(8,128)S(1)} %bitcast_maximum_fusion.1, pred[512,512]{0,1:T(8,128)(4,1)S(1)} %iota_compare_fusion, f32[512,8]{0,1:T(8,128)S(1)} %fusion.48, bf16[512,128]{1,0:T(8,128)(2,1)S(1)} %copy-done.5), kind=kOutput, calls=%fused_computation.34 | convolution fusion | flops 546832384 | bytes 11960320 | tf_op jit(solution)/shard_map/gtu,ud->tgd/dot_general | solution.py:71
  92.5 4.4 fusion.54
  100.3 42.7 %reduce-scatter.2.cloned.1.call-done = f32[128,2048]{1,0:T(8,128)} async-done(((f32[512,2048]{1,0:T(8,128)}), f32[128,2048]{1,0:T(8,128)}) %reduce-scatter.2.cloned.1.call-update) | async-done | bytes 1048592 | tf_op jit(solution)/shard_map/reduce_scatter | solution.py:86
  143.0 1.6 fusion.32
  146.4 26.0 %scatter_custom_fusion = bf16[2048,2048]{1,0:T(8,128)(2,1)} fusion(s32[1024]{0:T(1024)S(1)} %get-tuple-element.24, bf16[128,2048]{1,0:T(8,128)(2,1)} %fusion.34, s32[1024]{0:T(1024)S(1)} %get-tuple-element.23, bf16[]{:T(256)} %constant.49.clone.1), kind=kCustom, calls=%fused_computation.23 | custom fusion | bytes 8389120
  172.4 104.5 %all_to_all.10 = bf16[128,16,2048]{2,1,0:T(8,128)(2,1)S(1)} all-to-all(bf16[128,16,2048]{2,1,0:T(8,128)(2,1)} %bitcast.117), channel_id=1, replica_groups=mesh['ctx'=32,'head'=4] {'ctx','head'}, dimensions={0} | all-to-all | bytes 16777216 | tf_op jit(solution)/shard_map/all_to_all | solution.py:113
  276.9 35.8 %fusion.5 = f32[1,128,16,1536]{3,1,2,0:T(8,128)S(1)} fusion(bf16[128,16,2048]{2,1,0:T(8,128)(2,1)S(1)} %all_to_all.10, bf16[1,2048,1536]{2,1,0:T(8,128)(2,1)} %param.18), kind=kOutput, calls=%fused_computation.11 | convolution fusion | flops 12884901888 | bytes 27262976 | tf_op jit(solution)/shard_map/sekd,edf->eskf/dot_general | solution.py:18
  312.7 9.0 %convolution_convert_fusion = bf16[128,16,2048]{2,0,1:T(8,128)(2,1)} fusion(bf16[1,768,2048]{2,1,0:T(8,128)(2,1)S(1)} %copy-done, f32[1,128,16,1536]{3,1,2,0:T(8,128)S(1)} %fusion.5), kind=kOutput, calls=%fused_computation.20 | convolution fusion | flops 6456082432 | bytes 24117248 | tf_op jit(solution)/shard_map/eskf,efd->sekd/dot_general | solution.py:22
  321.7 11.2 %copy.52 = bf16[128,16,2048]{2,1,0:T(8,128)(2,1)} copy(bf16[128,16,2048]{2,0,1:T(8,128)(2,1)} %convolution_convert_fusion) | data formatting | bytes 16777216 | tf_op jit(solution)/shard_map/convert_element_type | solution.py:23
  332.9 6.9 %all-to-all-start.1 = ((bf16[128,16,2048]{2,1,0:T(8,128)(2,1)}), bf16[128,16,2048]{2,1,0:T(8,128)(2,1)}, u32[]{:S(2)}, u32[]{:S(2)}) async-start(bf16[128,16,2048]{2,1,0:T(8,128)(2,1)} %copy.52), calls=%async_computation.2 | async-start | bytes 16777216 | tf_op jit(solution)/shard_map/all_to_all | solution.py:118
  339.9 101.4 %all-to-all-done.1 = bf16[128,16,2048]{2,1,0:T(8,128)(2,1)} async-done(((bf16[128,16,2048]{2,1,0:T(8,128)(2,1)}), bf16[128,16,2048]{2,1,0:T(8,128)(2,1)}, u32[]{:S(2)}, u32[]{:S(2)}) %all-to-all-start.1) | async-done | bytes 8388640 | tf_op jit(solution)/shard_map/all_to_all | solution.py:118
  441.3 25.6 %gather_fusion = bf16[1024,2048]{1,0:T(8,128)(2,1)} fusion(bf16[128,16,2048]{2,1,0:T(8,128)(2,1)} %all-to-all-done.1, s32[1024]{0:T(1024)S(1)} %bitcast.116), kind=kCustom, calls=%fused_computation.1 | custom fusion | bytes 8396800 | tf_op jit(solution)/shard_map/gather | solution.py:119
  466.9 7.3 %fusion = bf16[128,2048]{1,0:T(8,128)(2,1)} fusion(bf16[1024,2048]{1,0:T(8,128)(2,1)} %gather_fusion, f32[128,8]{1,0:T(8,128)S(1)} %copy.45), kind=kLoop, calls=%fused_computation.4 | loop fusion | flops 6029312 | bytes 4722688 | tf_op jit(solution)/shard_map/reduce_sum | solution.py:121
  (59 shorter events, 9.0 us)
Async XLA Ops:
  7.2 305.6 %copy-start = (bf16[1,768,2048]{2,1,0:T(8,128)(2,1)S(1)}, bf16[1,768,2048]{2,1,0:T(8,128)(2,1)}, u32[]{:S(2)}) copy-start(bf16[1,768,2048]{2,1,0:T(8,128)(2,1)} %param.19) | copy-start | bytes 9437188
  7.2 59.5 %all-gather.2.cloned.1.call-start = ((), (), s32[]{:S(2)}) async-start(), calls=%async_computation.3 | async-start | bytes 8650752 | tf_op jit(solution)/shard_map/all_gather | solution.py:47
  9.1 133.9 %reduce-scatter.2.cloned.1.call-start = ((), (), s32[]{:S(2)}) async-start(), calls=%async_computation.4 | async-start | bytes 5242880 | tf_op jit(solution)/shard_map/reduce_scatter | solution.py:86
  78.4 8.4 %copy-start.5 = (bf16[512,128]{1,0:T(8,128)(2,1)S(1)}, bf16[512,128]{1,0:T(8,128)(2,1)}, u32[]{:S(2)}) copy-start(bf16[512,128]{1,0:T(8,128)(2,1)} %param.13) | copy-start | bytes 393220
  81.5 5.3 %copy-start.6 = (f32[8,4,128]{2,0,1:T(8,128)S(1)}, f32[8,4,128]{2,0,1:T(8,128)}, u32[]{:S(2)}) copy-start(f32[8,4,128]{2,0,1:T(8,128)} %get-tuple-element.9) | copy-start | bytes 49156
  81.5 5.3 %copy-start.4 = (f32[512,8,128]{0,2,1:T(8,128)S(1)}, f32[512,8,128]{0,2,1:T(8,128)}, u32[]{:S(2)}) copy-start(f32[512,8,128]{0,2,1:T(8,128)} %reshape.226) | copy-start | bytes 6291460
  86.8 5.7 %copy-start.1 = (bf16[1024,2048]{1,0:T(8,128)(2,1)S(1)}, bf16[1024,2048]{1,0:T(8,128)(2,1)}, u32[]{:S(2)}) copy-start(bf16[1024,2048]{1,0:T(8,128)(2,1)} %param.15) | copy-start | bytes 12582916
  92.5 4.4 copy-start.8
  96.9 3.2 copy-start.11
  96.9 3.3 copy-start.10
  96.9 48.5 %copy-start.7 = (f32[2048]{0:T(1024)S(1)}, f32[2048]{0:T(1024)}, u32[]{:S(2)}) copy-start(f32[2048]{0:T(1024)} %param.17) | copy-start | bytes 24580
  97.6 0.8 copy-start.2
  144.6 0.8 copy-start.3
  332.9 6.9 %copy-start.9 = (f32[128,8]{0,1:T(8,128)S(1)}, f32[128,8]{0,1:T(8,128)}, u32[]{:S(2)}) copy-start(f32[128,8]{0,1:T(8,128)} %param.21) | copy-start | bytes 12292
  332.9 108.4 %all-to-all-start.1 = ((bf16[128,16,2048]{2,1,0:T(8,128)(2,1)}), bf16[128,16,2048]{2,1,0:T(8,128)(2,1)}, u32[]{:S(2)}, u32[]{:S(2)}) async-start(bf16[128,16,2048]{2,1,0:T(8,128)(2,1)} %copy.52), calls=%async_computation.2 | async-start | bytes 16777216 | tf_op jit(solution)/shard_map/all_to_all | solution.py:118
Sparse Core Ops, SparseCore 0:
  10.8 55.7 all-gather.1
  97.1 45.8 reduce-scatter.1
where the time goes:
time: 488 us; the launch traced here: 481 us
  waiting for transfers between devices  183 us (38%)
  blocking collectives  105 us (22%)
  local copies, waits for them, and re-layouts  78.4 us (16%)
  matrix products  65.6 us (13%)
  other arithmetic  22.6 us (5%)
  between operations  20.6 us (4%)
  starting transfers between devices  6.97 us (1%)
    all_to_all x1, blocking collectives, body(): lax.all_to_all(outgoing, ('ctx', 'head'), split_axis=0, concat_axis=0, ti...  105 us
    all_to_all x1, waiting for transfers between devices, body(): lax.all_to_all(answered, ('ctx', 'head'), split_axis=0, concat_axis=0, ti...  101 us
    reduce_scatter x1, waiting for transfers between devices, body(): lax.psum_scatter(jnp.dot(attention, out_weight, preferred_element_type=jn...  42.7 us
    all_gather x1, waiting for transfers between devices, body(): everything = lax.all_gather(packed, 'ctx', axis=0, tiled=True)  38.7 us
    dot_general x1, matrix products, expert_rows(): jnp.einsum('sekd,edf->eskf', grid, expert_gate_up, preferred_element_type...  35.8 us
    unnamed x28, local copies, waits for them, and re-layouts  30.4 us
    gather x1, local copies, waits for them, and re-layouts, body(): picked = returned[flat_experts, places].astype(jnp.float32)  25.6 us
    convert_element_type x1, local copies, waits for them, and re-layouts, expert_rows(): return output.astype(jnp.bfloat16).reshape(arrived.shape)  11.2 us
  transfers between devices with their start and end apart: 3, of which 3 were waited for; matrix products, arithmetic and copies ran while one was open for 3% of the time, Pallas kernels for 0%

commit v1 on v0

--- a/solution.py
+++ b/solution.py
@@ -44,7 +44,9 @@
     source = lax.axis_index("ctx") - wanted
     usable = source >= 0
     packed = jnp.concatenate([keys, values], axis=1)
-    everything = lax.all_gather(packed, "ctx", axis=0, tiled=True)
+    carry = jnp.stack(tuple((packed for _ in range(lax.axis_size("ctx")))))
+    current_block = lax.all_to_all(carry, "ctx", 0, 0)
+    everything = jnp.concatenate(current_block, axis=0)
     offsets = jnp.maximum(source, 0) * length
     fetched = jnp.stack(
         [

time: 488 us -> 547 us (1.12)
  waiting for transfers between devices: 183 us -> 229 us
  starting transfers between devices: 6.97 us -> 15.9 us
    all_to_all x0 -> x1, waiting for transfers between devices: none -> 83.4 us  [body(): current_block = lax.all_to_all(carry, 'ctx', 0, 0)]
    all_gather x1 -> x0, waiting for transfers between devices: 38.7 us -> none  [body(): everything = lax.all_gather(packed, 'ctx', axis=0, tiled=True)]
    all_to_all x0 -> x1, starting transfers between devices: none -> 8.91 us  [body(): current_block = lax.all_to_all(carry, 'ctx', 0, 0)]
    unnamed x28 -> x36, local copies, waits for them, and re-layouts: 30.4 us -> 30 us
where the time goes in v1:
time: 547 us; the launch traced here: 540 us
  waiting for transfers between devices  229 us (42%)
  blocking collectives  105 us (19%)
  local copies, waits for them, and re-layouts  82.2 us (15%)
  matrix products  65.4 us (12%)
  other arithmetic  21.7 us (4%)
  between operations  20.7 us (4%)
  starting transfers between devices  15.9 us (3%)
    all_to_all x1, blocking collectives, body(): lax.all_to_all(outgoing, ('ctx', 'head'), split_axis=0, concat_axis=0, ti...  105 us
    all_to_all x1, waiting for transfers between devices, body(): lax.all_to_all(answered, ('ctx', 'head'), split_axis=0, concat_axis=0, ti...  101 us
    all_to_all x1, waiting for transfers between devices, body(): current_block = lax.all_to_all(carry, 'ctx', 0, 0)  83.4 us
    reduce_scatter x1, waiting for transfers between devices, body(): lax.psum_scatter(jnp.dot(attention, out_weight, preferred_element_type=jn...  44.4 us
    dot_general x1, matrix products, expert_rows(): jnp.einsum('sekd,edf->eskf', grid, expert_gate_up, preferred_element_type...  35.8 us
    unnamed x36, local copies, waits for them, and re-layouts  30 us
    gather x1, local copies, waits for them, and re-layouts, body(): picked = returned[flat_experts, places].astype(jnp.float32)  25.6 us
    convert_element_type x1, local copies, waits for them, and re-layouts, expert_rows(): return output.astype(jnp.bfloat16).reshape(arrived.shape)  11.2 us
  transfers between devices with their start and end apart: 3, of which 3 were waited for; matrix products, arithmetic and copies ran while one was open for 3% of the time, Pallas kernels for 0%

profile of v1, /device:TPU:7, one launch (start us, length us, event | category | flops | bytes accessed | tf_op | source)
XLA Modules:
  0.0 539.7 jit_solution(18380346977950944823)
XLA Ops:
  8.3 4.2 stack.10
  12.5 8.9 %all-to-all-start = ((bf16[32,512,256]{2,1,0:T(8,128)(2,1)}), bf16[32,512,256]{2,1,0:T(8,128)(2,1)}, u32[]{:S(2)}, u32[]{:S(2)}) async-start(bf16[32,512,256]{2,1,0:T(8,128)(2,1)} %stack.10), calls=%async_computation | async-start | bytes 16777216 | tf_op jit(solution)/shard_map/all_to_all | solution.py:48
  26.1 2.5 copy.69
  31.2 2.4 bitcast_bitcast_fusion
  33.6 5.9 %fusion.8 = (f32[8,512]{1,0:T(8,128)S(1)}, f32[512,512,8]{1,0,2:T(8,128)}) fusion(pred[512,512]{0,1:T(8,128)(4,1)S(1)} %iota_compare_fusion, bf16[512,128]{1,0:T(8,128)(2,1)S(1)} %copy-done.5, bf16[512,1024]{1,0:T(8,128)(2,1)} %param.11), kind=kOutput, calls=%fused_computation.12 | convolution fusion | flops 543158272 | bytes 9846784 | tf_op jit(solution)/shard_map/tgd,ud->gtu/dot_general | solution.py:59
  39.5 83.4 %all-to-all-done = bf16[32,512,256]{2,1,0:T(8,128)(2,1)} async-done(((bf16[32,512,256]{2,1,0:T(8,128)(2,1)}), bf16[32,512,256]{2,1,0:T(8,128)(2,1)}, u32[]{:S(2)}, u32[]{:S(2)}) %all-to-all-start) | async-done | bytes 8388640 | tf_op jit(solution)/shard_map/all_to_all | solution.py:48
  124.5 2.2 bitcast_reduce_fusion
  127.3 2.2 fusion.12
  129.6 2.5 fusion.27
  132.0 3.2 copy.44
  135.2 3.1 reshape.232
  138.3 5.3 fusion.3
  143.6 5.7 %fusion.26 = bf16[512,8,128]{0,2,1:T(8,128)(2,1)S(1)} fusion(f32[512,8,128]{0,2,1:T(8,128)S(1)} %copy-done.4, f32[512,512,8]{1,0,2:T(8,128)} %get-tuple-element.22, f32[8,512]{1,0:T(8,128)S(1)} %copy-done.7, pred[512,512]{0,1:T(8,128)(4,1)S(1)} %iota_compare_fusion, f32[512,8]{0,1:T(8,128)S(1)} %fusion.48, bf16[512,128]{1,0:T(8,128)(2,1)S(1)} %copy-done.6), kind=kOutput, calls=%fused_computation.34 | convolution fusion | flops 546832384 | bytes 11960320 | tf_op jit(solution)/shard_map/gtu,ud->tgd/dot_general | solution.py:73
  149.3 4.4 fusion.54
  157.1 44.4 %reduce-scatter.2.cloned.1.call-done = f32[128,2048]{1,0:T(8,128)} async-done(((f32[512,2048]{1,0:T(8,128)}), f32[128,2048]{1,0:T(8,128)}) %reduce-scatter.2.cloned.1.call-update) | async-done | bytes 1048592 | tf_op jit(solution)/shard_map/reduce_scatter | solution.py:88
  204.9 25.7 %scatter_custom_fusion = bf16[2048,2048]{1,0:T(8,128)(2,1)} fusion(s32[1024]{0:T(1024)S(1)} %get-tuple-element.24, bf16[128,2048]{1,0:T(8,128)(2,1)} %fusion.34, s32[1024]{0:T(1024)S(1)} %get-tuple-element.23, bf16[]{:T(256)} %constant.49.clone.1), kind=kCustom, calls=%fused_computation.23 | custom fusion | bytes 8389120
  230.6 104.5 %all_to_all.15 = bf16[128,16,2048]{2,1,0:T(8,128)(2,1)S(1)} all-to-all(bf16[128,16,2048]{2,1,0:T(8,128)(2,1)} %bitcast.118), channel_id=1, replica_groups=mesh['ctx'=32,'head'=4] {'ctx','head'}, dimensions={0} | all-to-all | bytes 16777216 | tf_op jit(solution)/shard_map/all_to_all | solution.py:115
  335.1 35.8 %fusion.5 = f32[1,128,16,1536]{3,1,2,0:T(8,128)S(1)} fusion(bf16[128,16,2048]{2,1,0:T(8,128)(2,1)S(1)} %all_to_all.15, bf16[1,2048,1536]{2,1,0:T(8,128)(2,1)} %param.18), kind=kOutput, calls=%fused_computation.11 | convolution fusion | flops 12884901888 | bytes 27262976 | tf_op jit(solution)/shard_map/sekd,edf->eskf/dot_general | solution.py:18
  370.9 8.9 %convolution_convert_fusion = bf16[128,16,2048]{2,0,1:T(8,128)(2,1)} fusion(bf16[1,768,2048]{2,1,0:T(8,128)(2,1)S(1)} %copy-done, f32[1,128,16,1536]{3,1,2,0:T(8,128)S(1)} %fusion.5), kind=kOutput, calls=%fused_computation.20 | convolution fusion | flops 6456082432 | bytes 24117248 | tf_op jit(solution)/shard_map/eskf,efd->sekd/dot_general | solution.py:22
  379.9 11.2 %copy.52 = bf16[128,16,2048]{2,1,0:T(8,128)(2,1)} copy(bf16[128,16,2048]{2,0,1:T(8,128)(2,1)} %convolution_convert_fusion) | data formatting | bytes 16777216 | tf_op jit(solution)/shard_map/convert_element_type | solution.py:23
  391.1 6.9 %all-to-all-start.2 = ((bf16[128,16,2048]{2,1,0:T(8,128)(2,1)}), bf16[128,16,2048]{2,1,0:T(8,128)(2,1)}, u32[]{:S(2)}, u32[]{:S(2)}) async-start(bf16[128,16,2048]{2,1,0:T(8,128)(2,1)} %copy.52), calls=%async_computation.3 | async-start | bytes 16777216 | tf_op jit(solution)/shard_map/all_to_all | solution.py:120
  398.1 101.4 %all-to-all-done.2 = bf16[128,16,2048]{2,1,0:T(8,128)(2,1)} async-done(((bf16[128,16,2048]{2,1,0:T(8,128)(2,1)}), bf16[128,16,2048]{2,1,0:T(8,128)(2,1)}, u32[]{:S(2)}, u32[]{:S(2)}) %all-to-all-start.2) | async-done | bytes 8388640 | tf_op jit(solution)/shard_map/all_to_all | solution.py:120
  499.5 25.6 %gather_fusion = bf16[1024,2048]{1,0:T(8,128)(2,1)} fusion(bf16[128,16,2048]{2,1,0:T(8,128)(2,1)} %all-to-all-done.2, s32[1024]{0:T(1024)S(1)} %bitcast.117), kind=kCustom, calls=%fused_computation.1 | custom fusion | bytes 8396800 | tf_op jit(solution)/shard_map/gather | solution.py:121
  525.1 7.3 %fusion = bf16[128,2048]{1,0:T(8,128)(2,1)} fusion(bf16[1024,2048]{1,0:T(8,128)(2,1)} %gather_fusion, f32[128,8]{1,0:T(8,128)S(1)} %copy.45), kind=kLoop, calls=%fused_computation.4 | loop fusion | flops 6029312 | bytes 4722688 | tf_op jit(solution)/shard_map/reduce_sum | solution.py:123
  (67 shorter events, 11.5 us)
Async XLA Ops:
  7.2 363.8 %copy-start = (bf16[1,768,2048]{2,1,0:T(8,128)(2,1)S(1)}, bf16[1,768,2048]{2,1,0:T(8,128)(2,1)}, u32[]{:S(2)}) copy-start(bf16[1,768,2048]{2,1,0:T(8,128)(2,1)} %param.19) | copy-start | bytes 9437188
  12.5 9.0 %copy-start.15 = (s32[1,3]{1,0:T(1,128)S(1)}, s32[1,3]{1,0:T(1,128)}, u32[]{:S(2)}) copy-start(s32[1,3]{1,0:T(1,128)} %param.14) | copy-start | bytes 40
  12.5 21.1 %copy-start.5 = (bf16[512,128]{1,0:T(8,128)(2,1)S(1)}, bf16[512,128]{1,0:T(8,128)(2,1)}, u32[]{:S(2)}) copy-start(bf16[512,128]{1,0:T(8,128)(2,1)} %param.12) | copy-start | bytes 393220
  12.5 110.4 %all-to-all-start = ((bf16[32,512,256]{2,1,0:T(8,128)(2,1)}), bf16[32,512,256]{2,1,0:T(8,128)(2,1)}, u32[]{:S(2)}, u32[]{:S(2)}) async-start(bf16[32,512,256]{2,1,0:T(8,128)(2,1)} %stack.10), calls=%async_computation | async-start | bytes 16777216 | tf_op jit(solution)/shard_map/all_to_all | solution.py:48
  21.4 180.1 %reduce-scatter.2.cloned.1.call-start = ((), (), s32[]{:S(2)}) async-start(), calls=%async_computation.4 | async-start | bytes 5242880 | tf_op jit(solution)/shard_map/reduce_scatter | solution.py:88
  124.3 3.0 copy-start.10
  129.6 8.7 %copy-start.7 = (f32[8,512]{1,0:T(8,128)S(1)}, f32[8,512]{1,0:T(8,128)}, u32[]{:S(2)}) copy-start(f32[8,512]{1,0:T(8,128)} %bitcast_maximum_fusion.1) | copy-start | bytes 49156
  135.2 8.4 %copy-start.6 = (bf16[512,128]{1,0:T(8,128)(2,1)S(1)}, bf16[512,128]{1,0:T(8,128)(2,1)}, u32[]{:S(2)}) copy-start(bf16[512,128]{1,0:T(8,128)(2,1)} %param.13) | copy-start | bytes 393220
  138.3 5.3 copy-start.8
  138.3 5.3 copy-start.4
  143.6 5.7 %copy-start.1 = (bf16[1024,2048]{1,0:T(8,128)(2,1)S(1)}, bf16[1024,2048]{1,0:T(8,128)(2,1)}, u32[]{:S(2)}) copy-start(bf16[1024,2048]{1,0:T(8,128)(2,1)} %param.15) | copy-start | bytes 12582916
  149.3 4.4 copy-start.11
  153.7 3.2 copy-start.14
  153.7 3.3 copy-start.13
  153.7 50.1 %copy-start.9 = (f32[2048]{0:T(1024)S(1)}, f32[2048]{0:T(1024)}, u32[]{:S(2)}) copy-start(f32[2048]{0:T(1024)} %param.17) | copy-start | bytes 24580
  154.5 0.8 copy-start.2
  203.1 0.8 copy-start.3
  391.1 6.9 %copy-start.12 = (f32[128,8]{0,1:T(8,128)S(1)}, f32[128,8]{0,1:T(8,128)}, u32[]{:S(2)}) copy-start(f32[128,8]{0,1:T(8,128)} %param.21) | copy-start | bytes 12292
  391.1 108.4 %all-to-all-start.2 = ((bf16[128,16,2048]{2,1,0:T(8,128)(2,1)}), bf16[128,16,2048]{2,1,0:T(8,128)(2,1)}, u32[]{:S(2)}, u32[]{:S(2)}) async-start(bf16[128,16,2048]{2,1,0:T(8,128)(2,1)} %copy.52), calls=%async_computation.3 | async-start | bytes 16777216 | tf_op jit(solution)/shard_map/all_to_all | solution.py:120
Sparse Core Ops, SparseCore 0:
  153.9 47.5 reduce-scatter.1
